TPU v7x, 256 devices: a whole 4x4x8 slice. The times are simulated.
256 devices in a mesh: row: 8 (over y, core), col: 32 (over z, x).
Axes of the slice: x: 4, y: 4, z: 8, core: 2. Of those that a mesh axis runs over, the one named last changes fastest.
Arguments:
- diag_block: float32 [1024, 1024], P('row')
- panel: bfloat16 [64, 1024, 1024], P('col', 'row'), may hold values from -1 to 1
- trailing: bfloat16 [32, 12, 1024, 1024], P('col', None, 'row'), may hold values from -6 to 6
- slot_rows: int32 [32, 12], replicated, may hold values from -1 to 63, as said below
- slot_cols: int32 [32, 12], replicated, may hold values from 0 to 1, as said below
Outputs:
- panel_factor: bfloat16 [64, 1024, 1024], P('col', 'row')
- updated: bfloat16 [32, 12, 1024, 1024], P('col', None, 'row')
Inputs may be any that keep to these rules, and one draw needn't show every extreme that they name: Slot s of grid column c holds the tile at tile row slot_rows[c, s] and tile column 2 * c + slot_cols[c, s] of the trailing matrix, or nothing where slot_rows[c, s] is -1. Live slots come first in each column; the pairs of one column are distinct and lie on or below the diagonal (tile row at least tile column). Within one grid column, live slots whose tile rows a and a' have a // 2 == a' // 2 have a == a'. Every column holds at least one live slot, column 0 fills all 12 slots and column 16 holds exactly one. `slot_cols`: 0 in empty slots.
All inputs are finite; a program needn't handle non-finite values.
Results may differ from a plain program's by a relative error of at most 0.0019.
Values may be sent and summed in bfloat16 or wider, within the bound.
No kernel may reach another device: no remote copies, remote signals or barrier semaphores. Data moves between devices by JAX's collectives and lax.ppermute only.
A program may use at most 128 MiB of HBM per device.

v0:
```python
import jax
import jax.numpy as jnp
from jax import lax
from jax.sharding import PartitionSpec as P


def slot_product(slices, left_ids, source_tiles, col_ids, position):
    left_slice = lax.dynamic_index_in_dim(slices, left_ids[position], 0, keepdims=False)
    right_tile = lax.dynamic_index_in_dim(source_tiles, col_ids[position], 0, keepdims=False)
    return lax.dot_general(
        left_slice, right_tile, (((1,), (1,)), ((), ())), preferred_element_type=jnp.float32
    )


def subtract_slot(buffer, position, update):
    previous = lax.dynamic_index_in_dim(buffer, position, 0, keepdims=False).astype(jnp.float32)
    return lax.dynamic_update_index_in_dim(
        buffer, (previous - update).astype(jnp.bfloat16), position, 0
    )


def local(diag_block, panel, trailing, slot_rows, slot_cols):
    diag_full = lax.all_gather(diag_block, "row", axis=0, tiled=True)
    factor = jnp.linalg.cholesky(diag_full)
    tile_count, row_count, tile_width = panel.shape
    stacked = panel.astype(jnp.float32).reshape(tile_count * row_count, tile_width)
    solved = lax.linalg.triangular_solve(factor, stacked.T, left_side=True, lower=True)
    panel_factor = solved.T.reshape(tile_count, row_count, tile_width).astype(jnp.bfloat16)
    whole_tiles = lax.all_gather(panel_factor, "row", axis=1, tiled=True)
    column_index = lax.axis_index("col")
    own_rows = lax.dynamic_index_in_dim(slot_rows, column_index, 0, keepdims=False)
    own_cols = lax.dynamic_index_in_dim(slot_cols, column_index, 0, keepdims=False)
    own_count = jnp.sum((own_rows >= 0).astype(jnp.int32))
    slices = lax.all_gather(panel_factor, "col", axis=0, tiled=True)

    def own_step(position, buffer):
        return subtract_slot(
            buffer, position, slot_product(slices, own_rows, whole_tiles, own_cols, position)
        )

    buffer = lax.fori_loop(0, own_count, own_step, trailing[0])
    return (panel_factor, buffer[None])


def solution(mesh):
    return jax.shard_map(
        local,
        mesh=mesh,
        in_specs=(P("row", None), P("col", "row", None), P("col", None, "row", None), P(), P()),
        out_specs=(P("col", "row", None), P("col", None, "row", None)),
        check_vma=False,
    )
```

profile of v0, /device:TPU:1, one launch (start us, length us, event | category | flops | bytes accessed | tf_op | source)
XLA Modules:
  0.0 681.8 jit_solution(6531067428901336610)
XLA Ops:
  9.6 43.7 %all-gather.4.cloned.1.call-done = f32[1024,1024]{0,1:T(8,128)} async-done(((f32[128,1024]{0,1:T(8,128)}), f32[1024,1024]{0,1:T(8,128)}) %all-gather.4.cloned.1.call-update) | async-done | bytes 4194320 | tf_op jit(solution)/shard_map/all_gather | solution.py:23
  53.3 5.3 copy.18
  58.7 4.4 fusion.18
  65.0 11.7 %cholesky.223 = f32[128,128]{1,0:T(8,128)S(1)} custom-call(f32[128,128]{1,0:T(8,128)S(1)} %cholesky.580), custom_call_target="Cholesky" | custom-call | tf_op jit(solution)/shard_map/jit(cholesky)/cholesky | solution.py:24
  76.8 9.8 %custom-call.62 = f32[1,128,128]{1,2,0:T(8,128)S(1)} custom-call(f32[1,128,128]{2,1,0:T(8,128)S(1)} %get-tuple-element.117), custom_call_target="InvertDiagBlocksLowerTriangular" | custom-call | tf_op jit(solution)/shard_map/jit(cholesky)/cholesky | solution.py:24
  93.0 12.2 %cholesky.244 = f32[128,128]{1,0:T(8,128)S(1)} custom-call(f32[128,128]{1,0:T(8,128)S(1)} %cholesky.584), custom_call_target="Cholesky" | custom-call | tf_op jit(solution)/shard_map/jit(cholesky)/cholesky | solution.py:24
  105.8 9.8 %custom-call.63 = f32[1,128,128]{1,2,0:T(8,128)S(1)} custom-call(f32[1,128,128]{2,1,0:T(8,128)S(1)} %get-tuple-element.114), custom_call_target="InvertDiagBlocksLowerTriangular" | custom-call | tf_op jit(solution)/shard_map/jit(cholesky)/cholesky | solution.py:24
  119.0 11.7 %cholesky.468 = f32[128,128]{1,0:T(8,128)S(1)} custom-call(f32[128,128]{1,0:T(8,128)S(1)} %cholesky.589), custom_call_target="Cholesky" | custom-call | tf_op jit(solution)/shard_map/jit(cholesky)/cholesky | solution.py:24
  132.0 9.8 %custom-call.64 = f32[1,128,128]{1,2,0:T(8,128)S(1)} custom-call(f32[1,128,128]{2,1,0:T(8,128)S(1)} %get-tuple-element.111), custom_call_target="InvertDiagBlocksLowerTriangular" | custom-call | tf_op jit(solution)/shard_map/jit(cholesky)/cholesky | solution.py:24
  145.3 11.8 %cholesky.487 = f32[128,128]{1,0:T(8,128)S(1)} custom-call(f32[128,128]{1,0:T(8,128)S(1)} %cholesky.594), custom_call_target="Cholesky" | custom-call | tf_op jit(solution)/shard_map/jit(cholesky)/cholesky | solution.py:24
  158.5 9.8 %custom-call.65 = f32[1,128,128]{1,2,0:T(8,128)S(1)} custom-call(f32[1,128,128]{2,1,0:T(8,128)S(1)} %get-tuple-element.108), custom_call_target="InvertDiagBlocksLowerTriangular" | custom-call | tf_op jit(solution)/shard_map/jit(cholesky)/cholesky | solution.py:24
  171.7 11.7 %cholesky.506 = f32[128,128]{1,0:T(8,128)S(1)} custom-call(f32[128,128]{1,0:T(8,128)S(1)} %cholesky.599), custom_call_target="Cholesky" | custom-call | tf_op jit(solution)/shard_map/jit(cholesky)/cholesky | solution.py:24
  184.7 10.0 %custom-call.66 = f32[1,128,128]{1,2,0:T(8,128)S(1)} custom-call(f32[1,128,128]{2,1,0:T(8,128)S(1)} %get-tuple-element.105), custom_call_target="InvertDiagBlocksLowerTriangular" | custom-call | tf_op jit(solution)/shard_map/jit(cholesky)/cholesky | solution.py:24
  198.1 11.7 %cholesky.526 = f32[128,128]{1,0:T(8,128)S(1)} custom-call(f32[128,128]{1,0:T(8,128)S(1)} %cholesky.604), custom_call_target="Cholesky" | custom-call | tf_op jit(solution)/shard_map/jit(cholesky)/cholesky | solution.py:24
  211.0 9.8 %custom-call.67 = f32[1,128,128]{1,2,0:T(8,128)S(1)} custom-call(f32[1,128,128]{2,1,0:T(8,128)S(1)} %get-tuple-element.102), custom_call_target="InvertDiagBlocksLowerTriangular" | custom-call | tf_op jit(solution)/shard_map/jit(cholesky)/cholesky | solution.py:24
  223.8 12.1 %cholesky.546 = f32[128,128]{1,0:T(8,128)S(1)} custom-call(f32[128,128]{1,0:T(8,128)S(1)} %cholesky.609), custom_call_target="Cholesky" | custom-call | tf_op jit(solution)/shard_map/jit(cholesky)/cholesky | solution.py:24
  237.2 9.8 %custom-call.68 = f32[1,128,128]{1,2,0:T(8,128)S(1)} custom-call(f32[1,128,128]{2,1,0:T(8,128)S(1)} %get-tuple-element.99), custom_call_target="InvertDiagBlocksLowerTriangular" | custom-call | tf_op jit(solution)/shard_map/jit(cholesky)/cholesky | solution.py:24
  249.7 11.7 %cholesky.564 = f32[128,128]{1,0:T(8,128)S(1)} custom-call(f32[128,128]{1,0:T(8,128)S(1)} %convolution_subtract_fusion.13), custom_call_target="Cholesky" | custom-call | tf_op jit(solution)/shard_map/jit(cholesky)/cholesky | solution.py:24
  268.3 4.8 select_select_fusion
  273.1 23.0 %while.12 = (s32[]{:T(128)}, f32[1024,1024]{1,0:T(8,128)}, s32[8,2]{0,1:T(2,128)S(1)}, f32[8,128,128]{2,1,0:T(8,128)S(1)}, s32[]{:T(128)}) while((s32[]{:T(128)}, f32[1024,1024]{1,0:T(8,128)}, s32[8,2]{0,1:T(2,128)S(1)}, f32[8,128,128]{2,1,0:T(8,128)S(1)}, s32[]{:T(128)}) %tuple.74), condition=%wide.while_cond, body=%wide.while_body.sunk | while | flops 2 | bytes 131189 | solution.py:27
  296.1 78.8 %custom-call.69 = f32[8,128,128]{1,2,0:T(8,128)S(1)} custom-call(f32[8,128,128]{2,1,0:T(8,128)S(1)} %get-tuple-element.48), custom_call_target="InvertDiagBlocksLowerTriangular" | custom-call | tf_op jit(solution)/shard_map/triangular_solve | solution.py:27
  398.6 34.2 %all-gather.8.cloned.1.call-done = bf16[2,1024,1024]{2,1,0:T(8,128)(2,1)} async-done(((bf16[2,128,1024]{2,1,0:T(8,128)(2,1)}), bf16[2,1024,1024]{2,1,0:T(8,128)(2,1)}) %all-gather.8.cloned.1.call-update) | async-done | bytes 4194320 | tf_op jit(solution)/shard_map/all_gather | solution.py:29
  432.8 142.9 %all-gather.6.cloned.1.call-done = bf16[64,128,1024]{2,1,0:T(8,128)(2,1)} async-done(((bf16[2,128,1024]{2,1,0:T(8,128)(2,1)}), bf16[64,128,1024]{2,1,0:T(8,128)(2,1)}) %all-gather.6.cloned.1.call-update) | async-done | bytes 16777232 | tf_op jit(solution)/shard_map/all_gather | solution.py:34
  575.8 97.6 %while.11 = (s32[]{:T(128)}, bf16[12,128,1024]{2,1,0:T(8,128)(2,1)S(1)}, s32[]{:T(128)}, s32[12]{0:T(128)S(1)}, bf16[64,128,1024]{2,1,0:T(8,128)(2,1)}, /*index=...) while((s32[]{:T(128)}, ...), condition=%wide.region_18.19_spmd, body=%wide.region_17.18_spmd.sunk | while | flops 268828672 | bytes 3408139 | solution.py:41
  (164 shorter events, 132.0 us)
Async XLA Ops:
  7.2 1.0 copy-start.4
  7.2 2.1 copy-start.5
  7.2 46.1 %all-gather.4.cloned.1.call-start = ((), (), s32[]{:S(2)}) async-start(), calls=%async_computation | async-start | bytes 4718592 | tf_op jit(solution)/shard_map/all_gather | solution.py:23
  9.2 423.6 %all-gather.8.cloned.1.call-start = ((), (), s32[]{:S(2)}) async-start(), calls=%async_computation.2 | async-start | bytes 4718592 | tf_op jit(solution)/shard_map/all_gather | solution.py:29
  9.6 372.6 %copy-start.3 = (f32[1024,256]{1,0:T(8,128)}, f32[1024,256]{1,0:T(8,128)S(1)}, u32[]{:S(2)}) copy-start(f32[1024,256]{1,0:T(8,128)S(1)} %bitcast_convert_fusion) | copy-start | bytes 3145732
  63.1 1.9 copy-start
  374.9 9.7 %copy-start.6 = (f32[8,128,128]{1,2,0:T(8,128)}, f32[8,128,128]{1,2,0:T(8,128)S(1)}, u32[]{:S(2)}) copy-start(f32[8,128,128]{1,2,0:T(8,128)S(1)} %custom-call.69) | copy-start | bytes 1572868
  384.7 13.1 %copy-start.7 = (s32[32,12]{0,1:T(8,128)S(1)}, s32[32,12]{0,1:T(8,128)}, u32[]{:S(2)}) copy-start(s32[32,12]{0,1:T(8,128)} %param.11) | copy-start | bytes 4612
  384.7 13.1 %copy-start.8 = (s32[32,12]{0,1:T(8,128)S(1)}, s32[32,12]{0,1:T(8,128)}, u32[]{:S(2)}) copy-start(s32[32,12]{0,1:T(8,128)} %param.10) | copy-start | bytes 4612
  384.7 191.1 %copy-start.2 = (bf16[1,12,128,1024]{3,2,1,0:T(8,128)(2,1)S(1)}, bf16[1,12,128,1024]{3,2,1,0:T(8,128)(2,1)}, u32[]{:S(2)}) copy-start(bf16[1,12,128,1024]{3,2,1,0:T(8,128)(2,1)} %param.9) | copy-start | bytes 9437188
  397.0 178.7 %all-gather.6.cloned.1.call-start = ((), (), s32[]{:S(2)}) async-start(), calls=%async_computation.1 | async-start | bytes 17301504 | tf_op jit(solution)/shard_map/all_gather | solution.py:34
  673.4 1.7 copy-start.1
Sparse Core Ops, SparseCore 0:
  10.4 42.8 all-gather.3
  397.1 35.6 all-gather.7
  436.0 139.6 all-gather.5
where the time goes:
time: 693 us; the launch traced here: 682 us
  other arithmetic  261 us (38%)
  waiting for transfers between devices  222 us (32%)
  matrix products  73.2 us (11%)
  local copies, waits for them, and re-layouts  53.5 us (8%)
  loops' own time  52.9 us (8%)
  between operations  19.3 us (3%)
    another operation x30, other arithmetic, local(): factor = jnp.linalg.cholesky(diag_full)  173 us
    all_gather x1, waiting for transfers between devices, local(): slices = lax.all_gather(panel_factor, 'col', axis=0, tiled=True)  143 us
    another operation x3, other arithmetic, local(): lax.linalg.triangular_solve(factor, stacked.T, left_side=True, lower=True)  83.6 us
    another operation x1, loops' own time, local(): buffer = lax.fori_loop(0, own_count, own_step, trailing[0])  52.7 us
    all_gather x1, waiting for transfers between devices, local(): diag_full = lax.all_gather(diag_block, 'row', axis=0, tiled=True)  43.7 us
    all_gather x1, waiting for transfers between devices, local(): whole_tiles = lax.all_gather(panel_factor, 'row', axis=1, tiled=True)  34.2 us
    dot_general x12, matrix products, slot_product(): lax.dot_general(left_slice, right_tile, (((1,), (1,)), ((), ())), preferr...  30.3 us
    another operation x14, matrix products, local(): factor = jnp.linalg.cholesky(diag_full)  23.1 us
  transfers between devices with their start and end apart: 3, of which 3 were waited for; matrix products, arithmetic and copies ran while one was open for 0% of the time, Pallas kernels for 0%

commit v1 on v0

--- a/solution.py
+++ b/solution.py
@@ -26,7 +26,15 @@
     stacked = panel.astype(jnp.float32).reshape(tile_count * row_count, tile_width)
     solved = lax.linalg.triangular_solve(factor, stacked.T, left_side=True, lower=True)
     panel_factor = solved.T.reshape(tile_count, row_count, tile_width).astype(jnp.bfloat16)
-    whole_tiles = lax.all_gather(panel_factor, "row", axis=1, tiled=True)
+    n_slots = lax.axis_size("row")
+    in_order = [(c, (c + 1) % n_slots) for c in range(n_slots)]
+    v_now = [None] * n_slots
+    v_now[n_slots - 1] = panel_factor
+    for w in range(n_slots - 2, -1, -1):
+        v_now[w] = lax.ppermute(v_now[w + 1], perm=in_order, axis_name="row")
+    now = jnp.concatenate(v_now, axis=1)
+    taken_in = (lax.axis_index("row") + 1) * panel_factor.shape[1]
+    whole_tiles = jnp.roll(now, taken_in, axis=1)
     column_index = lax.axis_index("col")
     own_rows = lax.dynamic_index_in_dim(slot_rows, column_index, 0, keepdims=False)
     own_cols = lax.dynamic_index_in_dim(slot_cols, column_index, 0, keepdims=False)

time: 693 us -> 647 us (0.934)
  waiting for transfers between devices: 222 us -> 161 us
  starting transfers between devices: 0.12 us -> 15.3 us
  matrix products: 73.2 us -> 65.5 us
    all_gather x1, waiting for transfers between devices: 143 us -> 72.3 us  [local(): slices = lax.all_gather(panel_factor, 'col', axis=0, tiled=True)]
    ppermute x0 -> x7, waiting for transfers between devices: none -> 45 us  [local(): v_now[w] = lax.ppermute(v_now[w + 1], perm=in_order, axis_name='row')]
    all_gather x1 -> x0, waiting for transfers between devices: 34.2 us -> none  [local(): whole_tiles = lax.all_gather(panel_factor, 'row', axis=1, tiled=True)]
    ppermute x0 -> x7, starting transfers between devices: none -> 15.2 us  [local(): v_now[w] = lax.ppermute(v_now[w + 1], perm=in_order, axis_name='row')]
    another operation x15, matrix products: 19.7 us -> 12 us  [local(): lax.linalg.triangular_solve(factor, stacked.T, left_side=True, lower=True)]
  transfers between devices with their start and end apart: 3 -> 9, of which waited for: 3 -> 9; matrix products, arithmetic and copies ran while one was open for 0% -> 1% of each run, Pallas kernels for 0% -> 0%
where the time goes in v1:
time: 647 us; the launch traced here: 635 us
  other arithmetic  261 us (40%)
  waiting for transfers between devices  161 us (25%)
  matrix products  65.5 us (10%)
  local copies, waits for them, and re-layouts  59.8 us (9%)
  loops' own time  52.9 us (8%)
  between operations  19.6 us (3%)
  starting transfers between devices  15.3 us (2%)
    another operation x30, other arithmetic, local(): factor = jnp.linalg.cholesky(diag_full)  172 us
    another operation x3, other arithmetic, local(): lax.linalg.triangular_solve(factor, stacked.T, left_side=True, lower=True)  83.6 us
    all_gather x1, waiting for transfers between devices, local(): slices = lax.all_gather(panel_factor, 'col', axis=0, tiled=True)  72.3 us
    another operation x1, loops' own time, local(): buffer = lax.fori_loop(0, own_count, own_step, trailing[0])  52.7 us
    ppermute x7, waiting for transfers between devices, local(): v_now[w] = lax.ppermute(v_now[w + 1], perm=in_order, axis_name='row')  45 us
    all_gather x1, waiting for transfers between devices, local(): diag_full = lax.all_gather(diag_block, 'row', axis=0, tiled=True)  43.7 us
    dot_general x12, matrix products, slot_product(): lax.dot_general(left_slice, right_tile, (((1,), (1,)), ((), ())), preferr...  30.3 us
    another operation x14, matrix products, local(): factor = jnp.linalg.cholesky(diag_full)  23.1 us
  transfers between devices with their start and end apart: 9, of which 9 were waited for; matrix products, arithmetic and copies ran while one was open for 1% of the time, Pallas kernels for 0%

profile of v1, /device:TPU:1, one launch (start us, length us, event | category | flops | bytes accessed | tf_op | source)
XLA Modules:
  0.0 635.4 jit_solution(8266441189054497562)
XLA Ops:
  9.6 43.7 %all-gather.3.cloned.1.call-done = f32[1024,1024]{0,1:T(8,128)} async-done(((f32[128,1024]{0,1:T(8,128)}), f32[1024,1024]{0,1:T(8,128)}) %all-gather.3.cloned.1.call-update) | async-done | bytes 4194320 | tf_op jit(solution)/shard_map/all_gather | solution.py:23
  65.0 11.7 %cholesky.223 = f32[128,128]{1,0:T(8,128)S(1)} custom-call(f32[128,128]{1,0:T(8,128)S(1)} %cholesky.580), custom_call_target="Cholesky" | custom-call | tf_op jit(solution)/shard_map/jit(cholesky)/cholesky | solution.py:24
  76.8 9.8 %custom-call.62 = f32[1,128,128]{1,2,0:T(8,128)S(1)} custom-call(f32[1,128,128]{2,1,0:T(8,128)S(1)} %get-tuple-element.117), custom_call_target="InvertDiagBlocksLowerTriangular" | custom-call | tf_op jit(solution)/shard_map/jit(cholesky)/cholesky | solution.py:24
  93.0 12.2 %cholesky.244 = f32[128,128]{1,0:T(8,128)S(1)} custom-call(f32[128,128]{1,0:T(8,128)S(1)} %cholesky.584), custom_call_target="Cholesky" | custom-call | tf_op jit(solution)/shard_map/jit(cholesky)/cholesky | solution.py:24
  105.8 9.8 %custom-call.63 = f32[1,128,128]{1,2,0:T(8,128)S(1)} custom-call(f32[1,128,128]{2,1,0:T(8,128)S(1)} %get-tuple-element.114), custom_call_target="InvertDiagBlocksLowerTriangular" | custom-call | tf_op jit(solution)/shard_map/jit(cholesky)/cholesky | solution.py:24
  119.0 11.7 %cholesky.468 = f32[128,128]{1,0:T(8,128)S(1)} custom-call(f32[128,128]{1,0:T(8,128)S(1)} %cholesky.589), custom_call_target="Cholesky" | custom-call | tf_op jit(solution)/shard_map/jit(cholesky)/cholesky | solution.py:24
  132.0 9.8 %custom-call.64 = f32[1,128,128]{1,2,0:T(8,128)S(1)} custom-call(f32[1,128,128]{2,1,0:T(8,128)S(1)} %get-tuple-element.111), custom_call_target="InvertDiagBlocksLowerTriangular" | custom-call | tf_op jit(solution)/shard_map/jit(cholesky)/cholesky | solution.py:24
  145.4 11.8 %cholesky.487 = f32[128,128]{1,0:T(8,128)S(1)} custom-call(f32[128,128]{1,0:T(8,128)S(1)} %cholesky.594), custom_call_target="Cholesky" | custom-call | tf_op jit(solution)/shard_map/jit(cholesky)/cholesky | solution.py:24
  158.5 9.8 %custom-call.65 = f32[1,128,128]{1,2,0:T(8,128)S(1)} custom-call(f32[1,128,128]{2,1,0:T(8,128)S(1)} %get-tuple-element.108), custom_call_target="InvertDiagBlocksLowerTriangular" | custom-call | tf_op jit(solution)/shard_map/jit(cholesky)/cholesky | solution.py:24
  171.8 11.7 %cholesky.506 = f32[128,128]{1,0:T(8,128)S(1)} custom-call(f32[128,128]{1,0:T(8,128)S(1)} %cholesky.599), custom_call_target="Cholesky" | custom-call | tf_op jit(solution)/shard_map/jit(cholesky)/cholesky | solution.py:24
  184.8 10.0 %custom-call.66 = f32[1,128,128]{1,2,0:T(8,128)S(1)} custom-call(f32[1,128,128]{2,1,0:T(8,128)S(1)} %get-tuple-element.105), custom_call_target="InvertDiagBlocksLowerTriangular" | custom-call | tf_op jit(solution)/shard_map/jit(cholesky)/cholesky | solution.py:24
  198.1 11.7 %cholesky.526 = f32[128,128]{1,0:T(8,128)S(1)} custom-call(f32[128,128]{1,0:T(8,128)S(1)} %cholesky.604), custom_call_target="Cholesky" | custom-call | tf_op jit(solution)/shard_map/jit(cholesky)/cholesky | solution.py:24
  211.1 9.8 %custom-call.67 = f32[1,128,128]{1,2,0:T(8,128)S(1)} custom-call(f32[1,128,128]{2,1,0:T(8,128)S(1)} %get-tuple-element.102), custom_call_target="InvertDiagBlocksLowerTriangular" | custom-call | tf_op jit(solution)/shard_map/jit(cholesky)/cholesky | solution.py:24
  223.9 12.1 %cholesky.546 = f32[128,128]{1,0:T(8,128)S(1)} custom-call(f32[128,128]{1,0:T(8,128)S(1)} %cholesky.609), custom_call_target="Cholesky" | custom-call | tf_op jit(solution)/shard_map/jit(cholesky)/cholesky | solution.py:24
  237.2 9.8 %custom-call.68 = f32[1,128,128]{1,2,0:T(8,128)S(1)} custom-call(f32[1,128,128]{2,1,0:T(8,128)S(1)} %get-tuple-element.99), custom_call_target="InvertDiagBlocksLowerTriangular" | custom-call | tf_op jit(solution)/shard_map/jit(cholesky)/cholesky | solution.py:24
  249.6 11.7 %cholesky.564 = f32[128,128]{1,0:T(8,128)S(1)} custom-call(f32[128,128]{1,0:T(8,128)S(1)} %convolution_subtract_fusion.13), custom_call_target="Cholesky" | custom-call | tf_op jit(solution)/shard_map/jit(cholesky)/cholesky | solution.py:24
  273.0 23.0 %while.12 = (s32[]{:T(128)}, f32[1024,1024]{1,0:T(8,128)}, s32[8,2]{0,1:T(2,128)S(1)}, f32[8,128,128]{2,1,0:T(8,128)S(1)}, s32[]{:T(128)}) while((s32[]{:T(128)}, f32[1024,1024]{1,0:T(8,128)}, s32[8,2]{0,1:T(2,128)S(1)}, f32[8,128,128]{2,1,0:T(8,128)S(1)}, s32[]{:T(128)}) %tuple.73), condition=%wide.while_cond, body=%wide.while_body.sunk | while | flops 2 | bytes 131181 | solution.py:27
  296.0 78.8 %custom-call.69 = f32[8,128,128]{1,2,0:T(8,128)S(1)} custom-call(f32[8,128,128]{2,1,0:T(8,128)S(1)} %get-tuple-element.48), custom_call_target="InvertDiagBlocksLowerTriangular" | custom-call | tf_op jit(solution)/shard_map/triangular_solve | solution.py:27
  389.2 6.4 %collective-permute-done = bf16[2,128,1024]{2,1,0:T(8,128)(2,1)S(1)} collective-permute-done((bf16[2,128,1024]{2,1,0:T(8,128)(2,1)}, bf16[2,128,1024]{2,1,0:T(8,128)(2,1)S(1)}, u32[]{:S(2)}, u32[]{:S(2)}) %collective-permute-start) | collective-permute-done | bytes 524320 | tf_op jit(solution)/shard_map/ppermute | solution.py:34
  406.6 6.1 collective-permute-done.2
  432.4 6.8 %collective-permute-done.5 = bf16[2,128,1024]{2,1,0:T(8,128)(2,1)} collective-permute-done((bf16[2,128,1024]{2,1,0:T(8,128)(2,1)S(1)}, bf16[2,128,1024]{2,1,0:T(8,128)(2,1)}, u32[]{:S(2)}, u32[]{:S(2)}) %collective-permute-start.5) | collective-permute-done | bytes 524320 | tf_op jit(solution)/shard_map/ppermute | solution.py:34
  442.2 7.2 %collective-permute-done.6 = bf16[2,128,1024]{2,1,0:T(8,128)(2,1)} collective-permute-done((bf16[2,128,1024]{2,1,0:T(8,128)(2,1)}, bf16[2,128,1024]{2,1,0:T(8,128)(2,1)}, u32[]{:S(2)}, u32[]{:S(2)}) %collective-permute-start.6) | collective-permute-done | bytes 524320 | tf_op jit(solution)/shard_map/ppermute | solution.py:34
  456.7 72.3 %all-gather.5.cloned.1.call-done = bf16[64,128,1024]{2,1,0:T(8,128)(2,1)} async-done(((bf16[2,128,1024]{2,1,0:T(8,128)(2,1)}), bf16[64,128,1024]{2,1,0:T(8,128)(2,1)}) %all-gather.5.cloned.1.call-update) | async-done | bytes 16777232 | tf_op jit(solution)/shard_map/all_gather | solution.py:42
  529.0 97.6 %while.11 = (s32[]{:T(128)}, bf16[12,128,1024]{2,1,0:T(8,128)(2,1)S(1)}, s32[]{:T(128)}, s32[12]{0:T(128)S(1)}, bf16[64,128,1024]{2,1,0:T(8,128)(2,1)}, /*index=...) while((s32[]{:T(128)}, ...), condition=%wide.region_18.19_spmd, body=%wide.region_17.18_spmd.sunk | while | flops 268828672 | bytes 3408131 | solution.py:49
  (191 shorter events, 178.0 us)
Async XLA Ops:
  7.2 434.0 %copy-start = (s32[32,12]{0,1:T(8,128)S(1)}, s32[32,12]{0,1:T(8,128)}, u32[]{:S(2)}) copy-start(s32[32,12]{0,1:T(8,128)} %param.10) | copy-start | bytes 4612
  7.2 1.0 copy-start.5
  7.2 2.1 copy-start.6
  7.2 46.1 %all-gather.3.cloned.1.call-start = ((), (), s32[]{:S(2)}) async-start(), calls=%async_computation | async-start | bytes 4718592 | tf_op jit(solution)/shard_map/all_gather | solution.py:23
  9.2 519.8 %all-gather.5.cloned.1.call-start = ((), (), s32[]{:S(2)}) async-start(), calls=%async_computation.1 | async-start | bytes 17301504 | tf_op jit(solution)/shard_map/all_gather | solution.py:42
  63.1 1.9 copy-start.1
  381.4 59.9 %copy-start.7 = (s32[32,12]{0,1:T(8,128)S(1)}, s32[32,12]{0,1:T(8,128)}, u32[]{:S(2)}) copy-start(s32[32,12]{0,1:T(8,128)} %param.11) | copy-start | bytes 4612
  388.1 63.7 %copy-start.2 = (bf16[256,1024]{1,0:T(8,128)(2,1)S(1)}, bf16[256,1024]{1,0:T(8,128)(2,1)}, u32[]{:S(2)}) copy-start(bf16[256,1024]{1,0:T(8,128)(2,1)} %copy.30) | copy-start | bytes 1572868
  388.1 7.5 %collective-permute-start = (bf16[2,128,1024]{2,1,0:T(8,128)(2,1)}, bf16[2,128,1024]{2,1,0:T(8,128)(2,1)S(1)}, u32[]{:S(2)}, u32[]{:S(2)}) collective-permute-start(bf16[2,128,1024]{2,1,0:T(8,128)(2,1)} %bitcast.144), channel_id=1, source_target_pairs={{0,32},{32,64},{64,96},{96,128},{128,160},{160,192},{192,224},{224... | collective-permute-start | bytes 1572872 | tf_op jit(solution)/shard_map/ppermute | solution.py:34
  395.6 8.5 %collective-permute-start.1 = (bf16[2,128,1024]{2,1,0:T(8,128)(2,1)S(1)}, bf16[2,128,1024]{2,1,0:T(8,128)(2,1)S(1)}, u32[]{:S(2)}, u32[]{:S(2)}) collective-permute-start(bf16[2,128,1024]{2,1,0:T(8,128)(2,1)S(1)} %collective-permute-done), channel_id=1, source_target_pairs={{0,32},{32,64},{64,96},{96,128},{128,160},{160,192},{192,224},{224... | collective-permute-start | bytes 1572872 | tf_op jit(solution)/shard_map/ppermute | solution.py:34
  404.1 8.6 %collective-permute-start.2 = (bf16[2,128,1024]{2,1,0:T(8,128)(2,1)S(1)}, bf16[2,128,1024]{2,1,0:T(8,128)(2,1)S(1)}, u32[]{:S(2)}, u32[]{:S(2)}) collective-permute-start(bf16[2,128,1024]{2,1,0:T(8,128)(2,1)S(1)} %collective-permute-done.1), channel_id=1, source_target_pairs={{0,32},{32,64},{64,96},{96,128},{128,160},{160,192},{192,224},{224... | collective-permute-start | bytes 1572872 | tf_op jit(solution)/shard_map/ppermute | solution.py:34
  412.7 8.6 %collective-permute-start.3 = (bf16[2,128,1024]{2,1,0:T(8,128)(2,1)S(1)}, bf16[2,128,1024]{2,1,0:T(8,128)(2,1)S(1)}, u32[]{:S(2)}, u32[]{:S(2)}) collective-permute-start(bf16[2,128,1024]{2,1,0:T(8,128)(2,1)S(1)} %collective-permute-done.2), channel_id=1, source_target_pairs={{0,32},{32,64},{64,96},{96,128},{128,160},{160,192},{192,224},{224... | collective-permute-start | bytes 1572872 | tf_op jit(solution)/shard_map/ppermute | solution.py:34
  421.3 8.6 %collective-permute-start.4 = (bf16[2,128,1024]{2,1,0:T(8,128)(2,1)S(1)}, bf16[2,128,1024]{2,1,0:T(8,128)(2,1)S(1)}, u32[]{:S(2)}, u32[]{:S(2)}) collective-permute-start(bf16[2,128,1024]{2,1,0:T(8,128)(2,1)S(1)} %collective-permute-done.3), channel_id=1, source_target_pairs={{0,32},{32,64},{64,96},{96,128},{128,160},{160,192},{192,224},{224... | collective-permute-start | bytes 1572872 | tf_op jit(solution)/shard_map/ppermute | solution.py:34
  429.9 9.3 %collective-permute-start.5 = (bf16[2,128,1024]{2,1,0:T(8,128)(2,1)S(1)}, bf16[2,128,1024]{2,1,0:T(8,128)(2,1)}, u32[]{:S(2)}, u32[]{:S(2)}) collective-permute-start(bf16[2,128,1024]{2,1,0:T(8,128)(2,1)S(1)} %collective-permute-done.4), channel_id=1, source_target_pairs={{0,32},{32,64},{64,96},{96,128},{128,160},{160,192},{192,224},{224... | collective-permute-start | bytes 1572872 | tf_op jit(solution)/shard_map/ppermute | solution.py:34
  439.3 10.1 %collective-permute-start.6 = (bf16[2,128,1024]{2,1,0:T(8,128)(2,1)}, bf16[2,128,1024]{2,1,0:T(8,128)(2,1)}, u32[]{:S(2)}, u32[]{:S(2)}) collective-permute-start(bf16[2,128,1024]{2,1,0:T(8,128)(2,1)} %collective-permute-done.5), channel_id=1, source_target_pairs={{0,32},{32,64},{64,96},{96,128},{128,160},{160,192},{192,224},{224... | collective-permute-start | bytes 1572872 | tf_op jit(solution)/shard_map/ppermute | solution.py:34
  454.3 74.7 %copy-start.4 = (bf16[1,12,128,1024]{3,2,1,0:T(8,128)(2,1)S(1)}, bf16[1,12,128,1024]{3,2,1,0:T(8,128)(2,1)}, u32[]{:S(2)}) copy-start(bf16[1,12,128,1024]{3,2,1,0:T(8,128)(2,1)} %param.9) | copy-start | bytes 9437188
  626.7 1.7 copy-start.3
Sparse Core Ops, SparseCore 0:
  10.4 42.8 all-gather.2
  388.3 140.7 all-gather.4
